TPU v7x, 32 devices: a whole 2x2x4 slice. The times are simulated.
32 devices in a mesh: groups: 2 (over x), section: 16 (over z, y, core).
Axes of the slice: x: 2, y: 2, z: 4, core: 2. Of those that a mesh axis runs over, the one named last changes fastest.
Arguments:
- micro: bfloat16 [32, 192, 1024], P(('groups', 'section')), parts along dimension 0, may hold values from -6 to 6
- segment: int32 [32, 192], P(('groups', 'section')), parts along dimension 0, may hold values from 0 to 3, as said below
- gain: bfloat16 [16, 1024], P('section'), may hold values from 0.099609375 to 1.8984375
- w_query: bfloat16 [16, 1024, 2048], P('section'), may hold values from -0.1875 to 0.1875
- w_key: bfloat16 [16, 1024, 1024], P('section'), may hold values from -0.1875 to 0.1875
- w_value: bfloat16 [16, 1024, 1024], P('section'), may hold values from -0.1875 to 0.1875
- w_out: bfloat16 [16, 2048, 1024], P('section'), may hold values from -0.125 to 0.125
Outputs:
- result: bfloat16 [32, 192, 1024], P(('groups', 'section')), parts along dimension 0
There are 2 independent parts, one for each index of `groups`. A program takes and returns all parts, laid end to end along the dimension named above; an argument that names none is the same for every part. Nothing has to cross between parts.
Inputs may be any that keep to these rules, and one draw needn't show every extreme that they name: `segment`: in each micro-batch the ids never fall, each of the 4 pairs holds 24 to 96 consecutive tokens, and one pair holds exactly 96.
All inputs are finite; a program needn't handle non-finite values.
Results may differ from a plain program's by a relative error of at most 0.013.
Values may be sent and summed in bfloat16 or wider, within the bound.
A program may use at most 128 MiB of HBM per device.

v0:
```python
import jax
import jax.numpy as jnp
from jax import lax
from jax.sharding import PartitionSpec as P

HEADS = 16
KV_HEADS = 8
HD = 128
TICKS = 4


def passed_along(array, axis, by):
    length = lax.axis_size(axis)
    return lax.ppermute(array, axis, [(i, (i + by) % length) for i in range(length)])


def positions(pair_ids):
    length = pair_ids.shape[0]
    matched = pair_ids[:, None] == pair_ids[None, :]
    row_index = lax.broadcasted_iota(jnp.int32, (length, length), 0)
    column = lax.broadcasted_iota(jnp.int32, (length, length), 1)
    earlier = matched & (column < row_index)
    places = jnp.sum(earlier.astype(jnp.float32), axis=1)
    allowed = matched & (column <= row_index)
    return (places, allowed)


def rotate(values, places):
    middle = values.shape[2] // 2
    ladder = jnp.arange(middle, dtype=jnp.float32)
    spacing = 1000000.0 ** (-2.0 * ladder / (2 * middle))
    angles = places[:, None, None] * spacing[None, None, :]
    cosine = jnp.cos(angles)
    sine_part = jnp.sin(angles)
    front_part = values[:, :, :middle]
    second = values[:, :, middle:]
    return jnp.concatenate(
        [front_part * cosine - second * sine_part, second * cosine + front_part * sine_part], axis=2
    )


def project(stream, pair_ids, gain_row, wq_layer, wk_layer, wv_layer):
    length = stream.shape[0]
    stream_f = stream.astype(jnp.float32)
    scale = lax.rsqrt(jnp.mean(stream_f * stream_f, axis=1, keepdims=True) + 1e-05)
    normed = (stream_f * scale * gain_row.astype(jnp.float32)[None, :]).astype(jnp.bfloat16)
    places, allowed = positions(pair_ids)
    queries = rotate(
        jnp.dot(normed, wq_layer, preferred_element_type=jnp.float32).reshape(length, HEADS, HD),
        places,
    ).astype(jnp.bfloat16)
    key_rows = rotate(
        jnp.dot(normed, wk_layer, preferred_element_type=jnp.float32).reshape(length, KV_HEADS, HD),
        places,
    ).astype(jnp.bfloat16)
    value_rows = (
        jnp.dot(normed, wv_layer, preferred_element_type=jnp.float32)
        .reshape(length, KV_HEADS, HD)
        .astype(jnp.bfloat16)
    )
    grouped = queries.reshape(length, KV_HEADS, HEADS // KV_HEADS, HD)
    return (grouped, key_rows, value_rows, allowed)


def respond(stream, grouped, key_rows, value_rows, allowed, wo_layer, start, stop):
    scores = jnp.einsum("ikgd,jkd->kgij", grouped, key_rows, preferred_element_type=jnp.float32)
    scores = scores * HD ** (-0.5)
    expo = jnp.where(allowed[None, None], jnp.exp(scores), jnp.zeros_like(scores))
    totals = jnp.sum(expo, axis=3, keepdims=True)
    shares = (expo / totals).astype(jnp.bfloat16)
    mixed = jnp.einsum(
        "kgij,jkd->ikgd", shares, value_rows, preferred_element_type=jnp.float32
    ).astype(jnp.bfloat16)
    mixed = mixed.reshape(stop - start, HEADS * HD)
    update = jnp.dot(mixed, wo_layer, preferred_element_type=jnp.float32)
    return (stream.astype(jnp.float32) + update).astype(jnp.bfloat16)


def body(micro, segment, gain, w_query, w_key, w_value, w_out):
    stream = micro[0]
    pair_ids = segment[0]
    gain_row = gain[0]
    wq_layer = w_query[0]
    wk_layer = w_key[0]
    wv_layer = w_value[0]
    wo_layer = w_out[0]
    length = stream.shape[0]
    for tick_index in range(TICKS):
        grouped, key_rows, value_rows, allowed = project(
            stream, pair_ids, gain_row, wq_layer, wk_layer, wv_layer
        )
        final = tick_index == TICKS - 1
        stream = respond(stream, grouped, key_rows, value_rows, allowed, wo_layer, 0, length)
        if not final:
            stream, pair_ids = passed_along((stream, pair_ids), "section", 1)
    return stream[None]


def solution(mesh):
    in_specs = (
        P(("groups", "section"), None, None),
        P(("groups", "section"), None),
        P("section", None),
        P("section", None, None),
        P("section", None, None),
        P("section", None, None),
        P("section", None, None),
    )
    out_specs = P(("groups", "section"), None, None)
    return jax.shard_map(body, mesh=mesh, in_specs=in_specs, out_specs=out_specs, check_vma=False)
```

profile of v0, /device:TPU:0, one launch (start us, length us, event | category | flops | bytes accessed | tf_op | source)
XLA Modules:
  0.0 134.6 jit_solution(12451186994389322092)
XLA Ops:
  0.0 0.5 collective-permute-start.1
  0.5 0.9 convert_reduce_fusion.3
  1.4 0.8 compare_and_fusion.7
  2.3 0.7 mul.524
  3.0 6.5 %copy.50 = bf16[2048,1024]{1,0:T(8,128)(2,1)} copy(bf16[2048,1024]{0,1:T(8,128)(2,1)} %bitcast.257) | data formatting | bytes 8388608 | tf_op jit(solution)/shard_map/dot_general | solution.py:49
  9.4 0.2 fusion.88
  9.6 4.0 %copy.49 = bf16[1024,1024]{1,0:T(8,128)(2,1)} copy(bf16[1024,1024]{0,1:T(8,128)(2,1)} %bitcast.258) | data formatting | bytes 4194304 | tf_op jit(solution)/shard_map/dot_general | solution.py:53
  13.6 3.8 %fusion.166 = f32[192,16,128]{2,0,1:T(8,128)S(1)} fusion(bf16[16,128,1024]{2,1,0:T(8,128)(2,1)} %bitcast.249, bf16[1,192,1024]{2,1,0:T(8,128)(2,1)S(1)} %copy-done.8, f32[1024]{0:T(1024)S(1)} %bitcast.267, f32[192]{0:T(256)S(1)} %add_rsqrt_fusion.3), kind=kOutput, calls=%fused_computation.175 | convolution fusion | flops 806092800 | bytes 6165248 | tf_op jit(solution)/shard_map/dot_general | solution.py:49
  17.5 0.9 fusion.168
  18.4 2.6 %collective-permute-start.3 = (s32[192]{0:T(256)S(1)}, s32[192]{0:T(256)S(1)}, u32[]{:S(2)}, u32[]{:S(2)}) collective-permute-start(s32[192]{0:T(256)S(1)} %collective-permute-done.1), channel_id=1, source_target_pairs={{0,1},{1,2},{2,3},{3,4},{4,5},{5,6},{6,7},{7,8},{8,9},{9,10},{10,1... | collective-permute-start | bytes 2312 | tf_op jit(solution)/shard_map/ppermute | solution.py:14
  21.0 0.1 convert_reduce_fusion.2
  21.1 3.6 %collective-permute-done.3 = s32[192]{0:T(256)S(1)} collective-permute-done((s32[192]{0:T(256)S(1)}, s32[192]{0:T(256)S(1)}, u32[]{:S(2)}, u32[]{:S(2)}) %collective-permute-start.3) | collective-permute-done | bytes 800 | tf_op jit(solution)/shard_map/ppermute | solution.py:14
  24.7 0.1 convert_reduce_fusion.1
  24.8 5.6 %collective-permute-done.5 = s32[192]{0:T(256)S(1)} collective-permute-done((s32[192]{0:T(256)S(1)}, s32[192]{0:T(256)S(1)}, u32[]{:S(2)}, u32[]{:S(2)}) %collective-permute-start.5) | collective-permute-done | bytes 800 | tf_op jit(solution)/shard_map/ppermute | solution.py:14
  30.4 0.1 convert_reduce_fusion
  30.5 2.1 %multiply_cosine_fusion = (f32[192,64]{1,0:T(8,128)S(1)}, f32[192,64]{1,0:T(8,128)S(1)}, f32[192,64]{1,0:T(8,128)}, f32[192,64]{1,0:T(8,128)}, f32[192,64]{1,0:T...) fusion(f32[192]{0:T(256)S(1)} %convert_reduce_fusion, f32[64]{0:T(128)S(1)} %multiply_power_fusion, ...), kind=kLoop, calls=%fused_computation.145 | loop fusion | flops 49152 | bytes 396544 | tf_op jit(solution)/shard_map/cos | solution.py:33
  32.6 0.6 subtract_convert_fusion.3
  33.2 0.4 subtract_convert_fusion.7
  33.6 2.9 %fusion.8 = (f32[8,2,192]{2,1,0:T(2,128)S(1)}, f32[8,192,192,2]{2,1,3,0:T(8,128)}) fusion(pred[192,192]{0,1:T(8,128)(4,1)S(1)} %compare_and_fusion.7, bf16[192,8,2,64]{3,0,2,1:T(8,128)(2,1)S(1)} %bitcast.260, bf16[192,8,2,64]{3,0,2,1:T(8,128)(2,1)S(1)} %bitcast.259, bf16[192,8,64]{2,0,1:T(8,128)(2,1)S(1)} %get-tuple-element.20, ...), kind=kOutput, calls=%fused_computation.16 | convolution fusion | flops 155120640 | bytes 3588096 | tf_op jit(solution)/shard_map/ikgd,jkd->kgij/dot_general | solution.py:66
  36.5 4.2 %fusion.32 = bf16[192,8,2,128]{3,0,2,1:T(8,128)(2,1)} fusion(f32[8,192,192,2]{2,1,3,0:T(8,128)} %get-tuple-element.36, f32[8,2,192]{2,1,0:T(2,128)S(1)} %get-tuple-element.35, pred[192,192]{0,1:T(8,128)(4,1)S(1)} %compare_and_fusion.7, bf16[1,192,1024]{2,1,0:T(8,128)(2,1)S(1)} %copy-done.8, f32[1024]{0:T(1024)S(1)} %bitcast.269, ...), kind=kOutput, calls=%fused_computation.48 | convolution fusion | flops 557383680 | bytes 5690112 | tf_op jit(solution)/shard_map/kgij,jkd->ikgd/dot_general | solution.py:71
  40.7 1.9 %copy.23 = bf16[192,8,2,128]{3,2,1,0:T(2,128)(2,1)S(1)} copy(bf16[192,8,2,128]{3,0,2,1:T(8,128)(2,1)} %fusion.32) | data formatting | bytes 1572864 | tf_op jit(solution)/shard_map/convert_element_type | solution.py:73
  42.6 1.5 %reshape.486 = bf16[192,2048]{1,0:T(8,128)(2,1)} reshape(bf16[192,8,2,128]{3,2,1,0:T(2,128)(2,1)S(1)} %copy.23) | data formatting | bytes 1572864 | tf_op jit(solution)/shard_map/reshape | solution.py:74
  44.1 3.6 %fusion.57 = bf16[192,1024]{1,0:T(8,128)(2,1)S(1)} fusion(bf16[192,2048]{1,0:T(8,128)(2,1)} %reshape.486, bf16[1,2048,1024]{2,1,0:T(8,128)(2,1)} %param.13, bf16[1,192,1024]{2,1,0:T(8,128)(2,1)S(1)} %copy-done.8), kind=kOutput, calls=%fused_computation.59 | convolution fusion | flops 805896192 | bytes 5767168 | tf_op jit(solution)/shard_map/dot_general | solution.py:75
  47.7 0.2 collective-permute-start
  47.9 0.1 compare_and_fusion.5
  48.0 9.8 %collective-permute-done = bf16[192,1024]{1,0:T(8,128)(2,1)S(1)} collective-permute-done((bf16[192,1024]{1,0:T(8,128)(2,1)S(1)}, bf16[192,1024]{1,0:T(8,128)(2,1)S(1)}, u32[]{:S(2)}, u32[]{:S(2)}) %collective-permute-start) | collective-permute-done | bytes 393248 | tf_op jit(solution)/shard_map/ppermute | solution.py:14
  57.8 0.2 fusion.91
  58.0 0.9 fusion.138
  58.9 0.4 subtract_convert_fusion.6
  59.3 0.9 copy-done.1
  60.2 1.5 %fusion.136 = f32[192,16,128]{2,0,1:T(8,128)S(1)} fusion(bf16[16,128,1024]{2,1,0:T(8,128)(2,1)S(1)} %bitcast.250, bf16[192,1024]{1,0:T(8,128)(2,1)S(1)} %collective-permute-done, f32[1024]{0:T(1024)S(1)} %bitcast.271, f32[192]{0:T(256)S(1)} %add_rsqrt_fusion.2), kind=kOutput, calls=%fused_computation.152 | convolution fusion | flops 806092800 | bytes 6165248 | tf_op jit(solution)/shard_map/dot_general | solution.py:49
  61.7 0.6 subtract_convert_fusion.2
  62.3 2.9 %fusion.9 = (f32[8,2,192]{2,1,0:T(2,128)S(1)}, f32[8,192,192,2]{2,1,3,0:T(8,128)}) fusion(pred[192,192]{0,1:T(8,128)(4,1)S(1)} %compare_and_fusion.5, bf16[192,8,2,64]{3,0,2,1:T(8,128)(2,1)S(1)} %bitcast.262, bf16[192,8,2,64]{3,0,2,1:T(8,128)(2,1)S(1)} %bitcast.261, bf16[192,8,64]{2,0,1:T(8,128)(2,1)S(1)} %get-tuple-element.18, ...), kind=kOutput, calls=%fused_computation.17 | convolution fusion | flops 155120640 | bytes 3588096 | tf_op jit(solution)/shard_map/ikgd,jkd->kgij/dot_general | solution.py:66
  65.3 4.2 %fusion.33 = bf16[192,8,2,128]{3,0,2,1:T(8,128)(2,1)} fusion(f32[8,192,192,2]{2,1,3,0:T(8,128)} %get-tuple-element.38, f32[8,2,192]{2,1,0:T(2,128)S(1)} %get-tuple-element.37, pred[192,192]{0,1:T(8,128)(4,1)S(1)} %compare_and_fusion.5, bf16[192,1024]{1,0:T(8,128)(2,1)S(1)} %collective-permute-done, f32[1024]{0:T(1024)S(1)} %bitcast.272, ...), kind=kOutput, calls=%fused_computation.49 | convolution fusion | flops 557383680 | bytes 5690112 | tf_op jit(solution)/shard_map/kgij,jkd->ikgd/dot_general | solution.py:71
  69.4 1.9 %copy.27 = bf16[192,8,2,128]{3,2,1,0:T(2,128)(2,1)S(1)} copy(bf16[192,8,2,128]{3,0,2,1:T(8,128)(2,1)} %fusion.33) | data formatting | bytes 1572864 | tf_op jit(solution)/shard_map/convert_element_type | solution.py:73
  71.4 1.5 %reshape.487 = bf16[192,2048]{1,0:T(8,128)(2,1)} reshape(bf16[192,8,2,128]{3,2,1,0:T(2,128)(2,1)S(1)} %copy.27) | data formatting | bytes 1572864 | tf_op jit(solution)/shard_map/reshape | solution.py:74
  72.9 3.6 %fusion.54 = bf16[192,1024]{1,0:T(8,128)(2,1)S(1)} fusion(bf16[192,2048]{1,0:T(8,128)(2,1)} %reshape.487, bf16[1,2048,1024]{2,1,0:T(8,128)(2,1)} %param.13, bf16[192,1024]{1,0:T(8,128)(2,1)S(1)} %collective-permute-done), kind=kOutput, calls=%fused_computation.58 | convolution fusion | flops 805896192 | bytes 5767168 | tf_op jit(solution)/shard_map/dot_general | solution.py:75
  76.4 0.3 collective-permute-start.2
  76.7 0.1 compare_and_fusion.3
  76.8 9.8 %collective-permute-done.2 = bf16[192,1024]{1,0:T(8,128)(2,1)S(1)} collective-permute-done((bf16[192,1024]{1,0:T(8,128)(2,1)S(1)}, bf16[192,1024]{1,0:T(8,128)(2,1)S(1)}, u32[]{:S(2)}, u32[]{:S(2)}) %collective-permute-start.2) | collective-permute-done | bytes 393248 | tf_op jit(solution)/shard_map/ppermute | solution.py:14
  86.6 0.2 fusion.94
  86.8 0.9 fusion.144
  87.7 0.4 subtract_convert_fusion.5
  88.1 0.9 copy-done.2
  89.0 1.5 %fusion.142 = f32[192,16,128]{2,0,1:T(8,128)S(1)} fusion(bf16[16,128,1024]{2,1,0:T(8,128)(2,1)S(1)} %bitcast.251, bf16[192,1024]{1,0:T(8,128)(2,1)S(1)} %collective-permute-done.2, f32[192]{0:T(256)S(1)} %add_rsqrt_fusion.1, f32[1024]{0:T(1024)S(1)} %bitcast.274), kind=kOutput, calls=%fused_computation.154 | convolution fusion | flops 806092800 | bytes 6165248 | tf_op jit(solution)/shard_map/dot_general | solution.py:49
  90.5 0.6 subtract_convert_fusion.1
  91.1 2.9 %fusion.10 = (f32[8,2,192]{2,1,0:T(2,128)S(1)}, f32[8,192,192,2]{2,1,3,0:T(8,128)}) fusion(pred[192,192]{0,1:T(8,128)(4,1)S(1)} %compare_and_fusion.3, bf16[192,8,2,64]{3,0,2,1:T(8,128)(2,1)S(1)} %bitcast.264, bf16[192,8,2,64]{3,0,2,1:T(8,128)(2,1)S(1)} %bitcast.263, bf16[192,8,64]{2,0,1:T(8,128)(2,1)S(1)} %get-tuple-element.16, ...), kind=kOutput, calls=%fused_computation.18 | convolution fusion | flops 155120640 | bytes 3588096 | tf_op jit(solution)/shard_map/ikgd,jkd->kgij/dot_general | solution.py:66
  94.1 4.2 %fusion.34 = bf16[192,8,2,128]{3,0,2,1:T(8,128)(2,1)} fusion(f32[8,192,192,2]{2,1,3,0:T(8,128)} %get-tuple-element.40, f32[8,2,192]{2,1,0:T(2,128)S(1)} %get-tuple-element.39, pred[192,192]{0,1:T(8,128)(4,1)S(1)} %compare_and_fusion.3, bf16[192,1024]{1,0:T(8,128)(2,1)S(1)} %collective-permute-done.2, f32[192]{0:T(256)S(1)} %add_rsqrt_fusion.1, ...), kind=kOutput, calls=%fused_computation.50 | convolution fusion | flops 557383680 | bytes 5690112 | tf_op jit(solution)/shard_map/kgij,jkd->ikgd/dot_general | solution.py:71
  98.2 1.9 %copy.31 = bf16[192,8,2,128]{3,2,1,0:T(2,128)(2,1)S(1)} copy(bf16[192,8,2,128]{3,0,2,1:T(8,128)(2,1)} %fusion.34) | data formatting | bytes 1572864 | tf_op jit(solution)/shard_map/convert_element_type | solution.py:73
  100.2 1.5 %reshape.488 = bf16[192,2048]{1,0:T(8,128)(2,1)} reshape(bf16[192,8,2,128]{3,2,1,0:T(2,128)(2,1)S(1)} %copy.31) | data formatting | bytes 1572864 | tf_op jit(solution)/shard_map/reshape | solution.py:74
  101.7 3.6 %fusion.51 = bf16[192,1024]{1,0:T(8,128)(2,1)S(1)} fusion(bf16[192,2048]{1,0:T(8,128)(2,1)} %reshape.488, bf16[1,2048,1024]{2,1,0:T(8,128)(2,1)} %param.13, bf16[192,1024]{1,0:T(8,128)(2,1)S(1)} %collective-permute-done.2), kind=kOutput, calls=%fused_computation.57 | convolution fusion | flops 805896192 | bytes 5767168 | tf_op jit(solution)/shard_map/dot_general | solution.py:75
  105.2 0.3 collective-permute-start.4
  105.7 9.8 %collective-permute-done.4 = bf16[192,1024]{1,0:T(8,128)(2,1)S(1)} collective-permute-done((bf16[192,1024]{1,0:T(8,128)(2,1)S(1)}, bf16[192,1024]{1,0:T(8,128)(2,1)S(1)}, u32[]{:S(2)}, u32[]{:S(2)}) %collective-permute-start.4) | collective-permute-done | bytes 393248 | tf_op jit(solution)/shard_map/ppermute | solution.py:14
  115.4 0.2 fusion.97
  115.6 0.9 fusion.150
  116.5 0.4 subtract_convert_fusion.4
  116.9 0.9 copy-done.3
  117.8 1.5 %fusion.148 = f32[192,16,128]{2,0,1:T(8,128)S(1)} fusion(bf16[16,128,1024]{2,1,0:T(8,128)(2,1)S(1)} %bitcast.252, bf16[192,1024]{1,0:T(8,128)(2,1)S(1)} %collective-permute-done.4, f32[192]{0:T(256)S(1)} %add_rsqrt_fusion, f32[1024]{0:T(1024)S(1)} %bitcast.277), kind=kOutput, calls=%fused_computation.156 | convolution fusion | flops 806092800 | bytes 6165248 | tf_op jit(solution)/shard_map/dot_general | solution.py:49
  119.3 0.6 subtract_convert_fusion
  120.0 2.9 %fusion.11 = (f32[8,2,192]{2,1,0:T(2,128)S(1)}, f32[8,192,192,2]{2,1,3,0:T(8,128)}) fusion(pred[192,192]{0,1:T(8,128)(4,1)S(1)} %compare_and_fusion.1, bf16[192,8,2,64]{3,0,2,1:T(8,128)(2,1)S(1)} %bitcast.266, bf16[192,8,2,64]{3,0,2,1:T(8,128)(2,1)S(1)} %bitcast.265, bf16[192,8,64]{2,0,1:T(8,128)(2,1)S(1)} %get-tuple-element.14, ...), kind=kOutput, calls=%fused_computation.19 | convolution fusion | flops 155120640 | bytes 3588096 | tf_op jit(solution)/shard_map/ikgd,jkd->kgij/dot_general | solution.py:66
  122.9 4.1 %fusion.35 = bf16[192,8,2,128]{3,0,2,1:T(8,128)(2,1)} fusion(f32[8,192,192,2]{2,1,3,0:T(8,128)} %get-tuple-element.42, f32[8,2,192]{2,1,0:T(2,128)S(1)} %get-tuple-element.41, pred[192,192]{0,1:T(8,128)(4,1)S(1)} %compare_and_fusion.1, bf16[192,1024]{1,0:T(8,128)(2,1)S(1)} %collective-permute-done.4, f32[192]{0:T(256)S(1)} %add_rsqrt_fusion, ...), kind=kOutput, calls=%fused_computation.51 | convolution fusion | flops 557383680 | bytes 5690112 | tf_op jit(solution)/shard_map/kgij,jkd->ikgd/dot_general | solution.py:71
  127.0 1.9 %copy.35 = bf16[192,8,2,128]{3,2,1,0:T(2,128)(2,1)S(1)} copy(bf16[192,8,2,128]{3,0,2,1:T(8,128)(2,1)} %fusion.35) | data formatting | bytes 1572864 | tf_op jit(solution)/shard_map/convert_element_type | solution.py:73
  129.0 1.5 %reshape.489 = bf16[192,2048]{1,0:T(8,128)(2,1)} reshape(bf16[192,8,2,128]{3,2,1,0:T(2,128)(2,1)S(1)} %copy.35) | data formatting | bytes 1572864 | tf_op jit(solution)/shard_map/reshape | solution.py:74
  130.5 4.2 %fusion.84 = bf16[1,192,1024]{2,1,0:T(8,128)(2,1)} fusion(bf16[192,2048]{1,0:T(8,128)(2,1)} %reshape.489, bf16[1,2048,1024]{2,1,0:T(8,128)(2,1)} %param.13, bf16[192,1024]{1,0:T(8,128)(2,1)S(1)} %collective-permute-done.4), kind=kOutput, calls=%fused_computation.68 | convolution fusion | flops 805896192 | bytes 5767168 | tf_op jit(solution)/shard_map/dot_general | solution.py:75
  (31 shorter events, 0.2 us)
Async XLA Ops:
  0.0 36.5 %copy-start = (bf16[1,1024,1024]{2,1,0:T(8,128)(2,1)S(1)}, bf16[1,1024,1024]{2,1,0:T(8,128)(2,1)}, u32[]{:S(2)}) copy-start(bf16[1,1024,1024]{2,1,0:T(8,128)(2,1)} %param.12) | copy-start | bytes 6291460
  0.0 18.4 %collective-permute-start.1 = (s32[192]{0:T(256)}, s32[192]{0:T(256)S(1)}, u32[]{:S(2)}, u32[]{:S(2)}) collective-permute-start(s32[192]{0:T(256)} %bitcast.279), channel_id=1, source_target_pairs={{0,1},{1,2},{2,3},{3,4},{4,5},{5,6},{6,7},{7,8},{8,9},{9,10},{10,1... | collective-permute-start | bytes 2312 | tf_op jit(solution)/shard_map/ppermute | solution.py:14
  3.0 6.5 %copy-start.8 = (bf16[1,192,1024]{2,1,0:T(8,128)(2,1)S(1)}, bf16[1,192,1024]{2,1,0:T(8,128)(2,1)}, u32[]{:S(2)}) copy-start(bf16[1,192,1024]{2,1,0:T(8,128)(2,1)} %param.7) | copy-start | bytes 1179652
  13.6 3.8 %copy-start.4 = (bf16[1024,1024]{1,0:T(8,128)(2,1)S(1)}, bf16[1024,1024]{1,0:T(8,128)(2,1)}, u32[]{:S(2)}) copy-start(bf16[1024,1024]{1,0:T(8,128)(2,1)} %copy.49) | copy-start | bytes 6291460
  18.4 6.3 %collective-permute-start.3 = (s32[192]{0:T(256)S(1)}, s32[192]{0:T(256)S(1)}, u32[]{:S(2)}, u32[]{:S(2)}) collective-permute-start(s32[192]{0:T(256)S(1)} %collective-permute-done.1), channel_id=1, source_target_pairs={{0,1},{1,2},{2,3},{3,4},{4,5},{5,6},{6,7},{7,8},{8,9},{9,10},{10,1... | collective-permute-start | bytes 2312 | tf_op jit(solution)/shard_map/ppermute | solution.py:14
  24.7 5.7 %collective-permute-start.5 = (s32[192]{0:T(256)S(1)}, s32[192]{0:T(256)S(1)}, u32[]{:S(2)}, u32[]{:S(2)}) collective-permute-start(s32[192]{0:T(256)S(1)} %collective-permute-done.3), channel_id=1, source_target_pairs={{0,1},{1,2},{2,3},{3,4},{4,5},{5,6},{6,7},{7,8},{8,9},{9,10},{10,1... | collective-permute-start | bytes 2312 | tf_op jit(solution)/shard_map/ppermute | solution.py:14
  44.1 13.9 %copy-start.5 = (bf16[1024,1024]{1,0:T(8,128)(2,1)S(1)}, bf16[1024,1024]{1,0:T(8,128)(2,1)}, u32[]{:S(2)}) copy-start(bf16[1024,1024]{1,0:T(8,128)(2,1)} %copy.49) | copy-start | bytes 6291460
  47.7 11.2 %copy-start.11 = (f32[192,64]{1,0:T(8,128)S(1)}, f32[192,64]{1,0:T(8,128)}, u32[]{:S(2)}) copy-start(f32[192,64]{1,0:T(8,128)} %get-tuple-element.29) | copy-start | bytes 147460
  47.7 11.2 %copy-start.12 = (f32[192,64]{1,0:T(8,128)S(1)}, f32[192,64]{1,0:T(8,128)}, u32[]{:S(2)}) copy-start(f32[192,64]{1,0:T(8,128)} %get-tuple-element.30) | copy-start | bytes 147460
  47.7 10.1 %collective-permute-start = (bf16[192,1024]{1,0:T(8,128)(2,1)S(1)}, bf16[192,1024]{1,0:T(8,128)(2,1)S(1)}, u32[]{:S(2)}, u32[]{:S(2)}) collective-permute-start(bf16[192,1024]{1,0:T(8,128)(2,1)S(1)} %fusion.57), channel_id=1, source_target_pairs={{0,1},{1,2},{2,3},{3,4},{4,5},{5,6},{6,7},{7,8},{8,9},{9,10},{10,1... | collective-permute-start | bytes 1179656 | tf_op jit(solution)/shard_map/ppermute | solution.py:14
  58.0 2.2 %copy-start.1 = (bf16[2048,1024]{1,0:T(8,128)(2,1)S(1)}, bf16[2048,1024]{1,0:T(8,128)(2,1)}, u32[]{:S(2)}) copy-start(bf16[2048,1024]{1,0:T(8,128)(2,1)} %copy.50) | copy-start | bytes 12582916
  72.9 13.9 %copy-start.6 = (bf16[1024,1024]{1,0:T(8,128)(2,1)S(1)}, bf16[1024,1024]{1,0:T(8,128)(2,1)}, u32[]{:S(2)}) copy-start(bf16[1024,1024]{1,0:T(8,128)(2,1)} %copy.49) | copy-start | bytes 6291460
  76.4 11.3 %copy-start.9 = (f32[192,64]{1,0:T(8,128)S(1)}, f32[192,64]{1,0:T(8,128)}, u32[]{:S(2)}) copy-start(f32[192,64]{1,0:T(8,128)} %get-tuple-element.31) | copy-start | bytes 147460
  76.4 11.3 %copy-start.10 = (f32[192,64]{1,0:T(8,128)S(1)}, f32[192,64]{1,0:T(8,128)}, u32[]{:S(2)}) copy-start(f32[192,64]{1,0:T(8,128)} %get-tuple-element.32) | copy-start | bytes 147460
  76.4 10.2 %collective-permute-start.2 = (bf16[192,1024]{1,0:T(8,128)(2,1)S(1)}, bf16[192,1024]{1,0:T(8,128)(2,1)S(1)}, u32[]{:S(2)}, u32[]{:S(2)}) collective-permute-start(bf16[192,1024]{1,0:T(8,128)(2,1)S(1)} %fusion.54), channel_id=1, source_target_pairs={{0,1},{1,2},{2,3},{3,4},{4,5},{5,6},{6,7},{7,8},{8,9},{9,10},{10,1... | collective-permute-start | bytes 1179656 | tf_op jit(solution)/shard_map/ppermute | solution.py:14
  86.8 2.2 %copy-start.2 = (bf16[2048,1024]{1,0:T(8,128)(2,1)S(1)}, bf16[2048,1024]{1,0:T(8,128)(2,1)}, u32[]{:S(2)}) copy-start(bf16[2048,1024]{1,0:T(8,128)(2,1)} %copy.50) | copy-start | bytes 12582916
  101.7 13.9 %copy-start.7 = (bf16[1024,1024]{1,0:T(8,128)(2,1)S(1)}, bf16[1024,1024]{1,0:T(8,128)(2,1)}, u32[]{:S(2)}) copy-start(bf16[1024,1024]{1,0:T(8,128)(2,1)} %copy.49) | copy-start | bytes 6291460
  105.2 10.2 %collective-permute-start.4 = (bf16[192,1024]{1,0:T(8,128)(2,1)S(1)}, bf16[192,1024]{1,0:T(8,128)(2,1)S(1)}, u32[]{:S(2)}, u32[]{:S(2)}) collective-permute-start(bf16[192,1024]{1,0:T(8,128)(2,1)S(1)} %fusion.51), channel_id=1, source_target_pairs={{0,1},{1,2},{2,3},{3,4},{4,5},{5,6},{6,7},{7,8},{8,9},{9,10},{10,1... | collective-permute-start | bytes 1179656 | tf_op jit(solution)/shard_map/ppermute | solution.py:14
  115.6 2.2 %copy-start.3 = (bf16[2048,1024]{1,0:T(8,128)(2,1)S(1)}, bf16[2048,1024]{1,0:T(8,128)(2,1)}, u32[]{:S(2)}) copy-start(bf16[2048,1024]{1,0:T(8,128)(2,1)} %copy.50) | copy-start | bytes 12582916
where the time goes:
time: 135 us
  matrix products  55.1 us (41%)
  waiting for transfers between devices  38.6 us (29%)
  local copies, waits for them, and re-layouts  26.9 us (20%)
  other arithmetic  9.81 us (7%)
  starting transfers between devices  3.93 us (3%)
    ppermute x6, waiting for transfers between devices, passed_along(): lax.ppermute(array, axis, [(i, (i + by) % length) for i in range(length)])  38.6 us
    dot_general x4, matrix products, respond(): jnp.einsum('kgij,jkd->ikgd', shares, value_rows, preferred_element_type=j...  16.6 us
    dot_general x4, matrix products, respond(): update = jnp.dot(mixed, wo_layer, preferred_element_type=jnp.float32)  14.8 us
    dot_general x4, matrix products, respond(): jnp.einsum('ikgd,jkd->kgij', grouped, key_rows, preferred_element_type=jn...  11.8 us
    dot_general x4, matrix products, project(): jnp.dot(normed, wq_layer, preferred_element_type=jnp.float32)  8.4 us
    convert_element_type x4, local copies, waits for them, and re-layouts, respond(): mixed = jnp.einsum('kgij,jkd->ikgd', shares, value_rows, preferred_elemen...  7.77 us
    dot_general x1, local copies, waits for them, and re-layouts, project(): jnp.dot(normed, wq_layer, preferred_element_type=jnp.float32)  6.45 us
    reshape x4, local copies, waits for them, and re-layouts, respond(): mixed = mixed.reshape(stop - start, HEADS * HD)  5.91 us
  transfers between devices with their start and end apart: 6, of which 5 were waited for; matrix products, arithmetic and copies ran while one was open for 14% of the time, Pallas kernels for 0%

commit v1 on v0

v1 whole, which is shorter than its diff:
```python
import functools
import math

import jax
import jax.numpy as jnp
import numpy as np
from jax import lax
from jax.experimental import pallas as pl
from jax.experimental.pallas import tpu as pltpu
from jax.sharding import PartitionSpec as P

HEADS = 16
KV_HEADS = 8
HD = 128
TICKS = 4
CUT = 96
BAND = 96
MESH = pl.DeviceIdType.MESH
GROUP = 4 * HD


def rope_table(length):
    spacing = 1000000.0 ** (-2.0 * np.arange(HD // 2) / HD)
    angles = np.arange(length)[:, None] * spacing[None, :]
    cosine, sine = np.cos(angles), np.sin(angles)
    full = np.concatenate([cosine, cosine, -sine, sine], axis=1).astype(np.float32)
    high = full.astype(jnp.bfloat16)
    low = (full - high.astype(np.float32)).astype(jnp.bfloat16)
    return np.concatenate([high, low], axis=1)


def blocks_of(start, stop):
    if start == 0:
        return [(0, stop, 0, stop)]
    rows = 128 - BAND
    return [(r, r + rows, r - BAND, r + rows) for r in range(start, stop, rows)]


def kernel(
    length, chunks,
    micro, ids, gain_hbm, table_hbm, wq, wk, wv, wo, out,
    xbuf, ybuf, idbuf, gain, table, wqkv, wout,
    normed, qs, ks, vs, mixed, cosine, sine, bias,
    wsem, osem, lsem, send, recv, id_send, id_recv,
):
    n = lax.axis_size("section")
    me = lax.axis_index("section")
    right, left = lax.rem(me + 1, n), lax.rem(me + n - 1, n)

    def local(src, dst, sem):
        return pltpu.make_async_copy(src, dst, sem)

    small = [
        local(ids, idbuf.at[0], lsem.at[0]),
        local(table_hbm, table, lsem.at[1]),
        local(micro.at[0], xbuf.at[0], lsem.at[2]),
        local(gain_hbm, gain, lsem.at[3]),
    ]
    for copy in small:
        copy.start()

    def group_copies(g):
        q_at = pl.ds(g * 2 * HD, 2 * HD)
        k_at = pl.ds(g * HD, HD)
        return (
            local(wq.at[0, :, q_at], wqkv.at[g, :, 0 : 2 * HD], wsem.at[g, 0]),
            local(wk.at[0, :, k_at], wqkv.at[g, :, 2 * HD : 3 * HD], wsem.at[g, 1]),
            local(wv.at[0, :, k_at], wqkv.at[g, :, 3 * HD :], wsem.at[g, 2]),
        )

    for g in range(KV_HEADS):
        for copy in group_copies(g):
            copy.start()
    out_copy = local(wo.at[0], wout, osem)
    out_copy.start()

    barrier = pltpu.get_barrier_semaphore()
    pl.semaphore_signal(barrier, inc=1, device_id={"section": left}, device_id_type=MESH)
    pl.semaphore_wait(barrier, 1)
    for copy in small:
        copy.wait()

    def rows_copy(t, c):
        at = pl.ds(chunks[c][0], chunks[c][1] - chunks[c][0])
        return pltpu.make_async_remote_copy(
            ybuf.at[t, at, :], xbuf.at[t + 1, at, :], send.at[t, c], recv.at[t, c],
            device_id={"section": right}, device_id_type=MESH,
        )

    def id_copy(t):
        return pltpu.make_async_remote_copy(
            idbuf.at[t], idbuf.at[t + 1], id_send.at[t], id_recv.at[t],
            device_id={"section": right}, device_id_type=MESH,
        )

    def places(t):
        row = idbuf[t].astype(jnp.float32)
        i = lax.broadcasted_iota(jnp.int32, (length, length), 0)
        j = lax.broadcasted_iota(jnp.int32, (length, length), 1)
        across = jnp.broadcast_to(row, (length, length))
        down = jnp.sum(jnp.where(i == j, across, 0.0), axis=1, keepdims=True)
        matched = across == down
        place = jnp.sum(jnp.where(matched & (j < i), 1.0, 0.0), axis=1, keepdims=True)
        chosen = jnp.where(j.astype(jnp.float32) == place, 1.0, 0.0).astype(jnp.bfloat16)
        turns = jnp.dot(chosen, table[...], preferred_element_type=jnp.float32)
        cosine[...] = turns[:, :HD] + turns[:, 2 * HD : 3 * HD]
        sine[...] = turns[:, HD : 2 * HD] + turns[:, 3 * HD :]
        limits = jnp.where(matched & (j <= i), 0.0, -1e30)
        for start, stop in chunks:
            for r0, r1, k0, k1 in blocks_of(start, stop):
                bias[r0:r1, 0 : k1 - k0] = limits[r0:r1, k0:k1]

    def turn(x, rows):
        return (x * cosine[rows, :] + pltpu.roll(x, HD // 2, 1) * sine[rows, :]).astype(jnp.bfloat16)

    def project(g, start, stop):
        rows = pl.ds(start, stop - start)
        return jnp.dot(normed[rows, :], wqkv[g], preferred_element_type=jnp.float32)

    def keep(g, start, stop, made):
        rows = pl.ds(start, stop - start)
        qs[g, 0, rows, :] = turn(made[:, :HD], rows)
        qs[g, 1, rows, :] = turn(made[:, HD : 2 * HD], rows)
        ks[g, rows, :] = turn(made[:, 2 * HD : 3 * HD], rows)
        vs[g, rows, :] = made[:, 3 * HD :].astype(jnp.bfloat16)

    def attend(g, start, stop):
        for r0, r1, k0, k1 in blocks_of(start, stop):
            count, width = r1 - r0, k1 - k0
            q = qs[g, :, r0:r1, :].reshape(2 * count, HD)
            scores = lax.dot_general(
                q, ks[g, k0:k1, :], (((1,), (1,)), ((), ())), preferred_element_type=jnp.float32
            ).reshape(2, count, width)
            expo = jnp.exp2(scores * (HD ** -0.5 * math.log2(math.e)) + bias[r0:r1, 0:width][None])
            shares = (expo / jnp.sum(expo, axis=2, keepdims=True)).astype(jnp.bfloat16)
            got = jnp.dot(
                shares.reshape(2 * count, width), vs[g, k0:k1, :], preferred_element_type=jnp.float32
            ).astype(jnp.bfloat16)
            both = jnp.concatenate([got[:count], got[count:]], axis=1)
            mixed[r0:r1, pl.ds(pl.multiple_of(g * 2 * HD, 2 * HD), 2 * HD)] = both

    def tick(t, first, waits):
        if not first:
            id_copy(t - 1).wait_recv()

        def forward():
            id_copy(t).start()

        if first:
            forward()
        else:
            pl.when(t < TICKS - 1)(forward)
        places(t)
        for c, (start, stop) in enumerate(chunks):
            rows = pl.ds(start, stop - start)
            if not first:
                rows_copy(t - 1, c).wait_recv()
            x = xbuf[t, rows, :].astype(jnp.float32)
            scale = lax.rsqrt(jnp.mean(x * x, axis=1, keepdims=True) + 1e-05)
            normed[rows, :] = (x * scale * gain[...].astype(jnp.float32)).astype(jnp.bfloat16)
            load = first and c == 0

            def ready(g):
                if load:
                    for copy in group_copies(g):
                        copy.wait()

            ready(0)
            keep(0, start, stop, project(0, start, stop))

            def step(g, carry):
                ready(g + 1)
                made = project(g + 1, start, stop)
                attend(g, start, stop)
                keep(g + 1, start, stop, made)
                return carry

            if load:
                for g in range(KV_HEADS - 1):
                    step(g, 0)
            else:
                lax.fori_loop(0, KV_HEADS - 1, step, 0)
            attend(KV_HEADS - 1, start, stop)
            if load:
                out_copy.wait()
            width = 256
            for at in range(0, ybuf.shape[2], width):
                update = jnp.dot(
                    mixed[rows, :], wout[:, at : at + width], preferred_element_type=jnp.float32
                )
                ybuf[t, rows, at : at + width] = (
                    xbuf[t, rows, at : at + width].astype(jnp.float32) + update
                ).astype(jnp.bfloat16)
            if first:
                rows_copy(t, c).start()
            else:
                pl.when(t < TICKS - 1)(rows_copy(t, c).start)

    tick(0, True, True)

    def later(t, carry):
        tick(t, False, False)
        return carry

    lax.fori_loop(1, TICKS, later, 0)
    out[0] = ybuf[TICKS - 1]
    for t in range(TICKS - 1):
        id_copy(t).wait_send()
        for c in range(len(chunks)):
            rows_copy(t, c).wait_send()


def body(micro, segment, gain, w_query, w_key, w_value, w_out):
    _, length, width = micro.shape
    chunks = [(0, CUT), (CUT, length)]
    table = jnp.asarray(rope_table(length))
    bf, f32 = jnp.bfloat16, jnp.float32
    count = len(chunks)
    any_space = pl.BlockSpec(memory_space=pl.ANY)
    vmem = pl.BlockSpec(memory_space=pltpu.VMEM)
    return pl.pallas_call(
        functools.partial(kernel, length, chunks),
        out_shape=jax.ShapeDtypeStruct((1, length, width), bf),
        in_specs=[any_space] * 8,
        out_specs=vmem,
        scratch_shapes=[
            pltpu.VMEM((TICKS, length, width), bf),
            pltpu.VMEM((TICKS, length, width), bf),
            pltpu.VMEM((TICKS, 1, length), jnp.int32),
            pltpu.VMEM((1, width), bf),
            pltpu.VMEM(table.shape, bf),
            pltpu.VMEM((KV_HEADS, width, GROUP), bf),
            pltpu.VMEM((HEADS * HD, width), bf),
            pltpu.VMEM((length, width), bf),
            pltpu.VMEM((KV_HEADS, 2, length, HD), bf),
            pltpu.VMEM((KV_HEADS, length, HD), bf),
            pltpu.VMEM((KV_HEADS, length, HD), bf),
            pltpu.VMEM((length, HEADS * HD), bf),
            pltpu.VMEM((length, HD), f32),
            pltpu.VMEM((length, HD), f32),
            pltpu.VMEM((length, HD), f32),
            pltpu.SemaphoreType.DMA((KV_HEADS, 3)),
            pltpu.SemaphoreType.DMA,
            pltpu.SemaphoreType.DMA((4,)),
            pltpu.SemaphoreType.DMA((TICKS - 1, count)),
            pltpu.SemaphoreType.DMA((TICKS - 1, count)),
            pltpu.SemaphoreType.DMA((TICKS - 1,)),
            pltpu.SemaphoreType.DMA((TICKS - 1,)),
        ],
        compiler_params=pltpu.CompilerParams(
            collective_id=0, has_side_effects=True, vmem_limit_bytes=60 * 1024 * 1024
        ),
    )(micro, segment, gain, table, w_query, w_key, w_value, w_out)


def solution(mesh):
    in_specs = (
        P(("groups", "section"), None, None),
        P(("groups", "section"), None),
        P("section", None),
        P("section", None, None),
        P("section", None, None),
        P("section", None, None),
        P("section", None, None),
    )
    out_specs = P(("groups", "section"), None, None)
    return jax.shard_map(body, mesh=mesh, in_specs=in_specs, out_specs=out_specs, check_vma=False)
```

time: 135 us -> 68.2 us (0.51)
  Pallas kernels: 0 us -> 66.3 us
  matrix products: 55.1 us -> 0 us
  waiting for transfers between devices: 38.6 us -> 0 us
  local copies, waits for them, and re-layouts: 26.9 us -> 1.77 us
  other arithmetic: 9.81 us -> 0 us
  starting transfers between devices: 3.93 us -> 0 us
    pallas_call x0 -> x1, Pallas kernels: none -> 66.3 us  [body(): pl.pallas_call(functools.partial(kernel, length, chunks), out_shape=jax.S...]
    dot_general x20 -> x0, matrix products: 55.1 us -> none  [the longest x4 16.6 us: respond(): jnp.einsum('kgij,jkd->ikgd', shares, value_rows, preferred_element_type=j...]
    ppermute x6 -> x0, waiting for transfers between devices: 38.6 us -> none  [passed_along(): lax.ppermute(array, axis, [(i, (i + by) % length) for i in range(length)])]
    dot_general x2 -> x0, local copies, waits for them, and re-layouts: 10.5 us -> none  [the longest x1 6.45 us: project(): jnp.dot(normed, wq_layer, preferred_element_type=jnp.float32)]
    convert_element_type x4 -> x0, local copies, waits for them, and re-layouts: 7.77 us -> none  [respond(): mixed = jnp.einsum('kgij,jkd->ikgd', shares, value_rows, preferred_elemen...]
    reshape x4 -> x0, local copies, waits for them, and re-layouts: 5.91 us -> none  [respond(): mixed = mixed.reshape(stop - start, HEADS * HD)]
    another operation x8 -> x0, other arithmetic: 3.98 us -> none
    ppermute x6 -> x0, starting transfers between devices: 3.93 us -> none  [passed_along(): lax.ppermute(array, axis, [(i, (i + by) % length) for i in range(length)])]
  transfers between devices with their start and end apart: 6 -> 0, of which waited for: 5 -> 0; matrix products, arithmetic and copies ran while one was open for 14% -> 0% of each run, Pallas kernels for 0% -> 0%
where the time goes in v1:
time: 68.2 us; the launch traced here: 68.1 us
  Pallas kernels  66.3 us (97%)
  local copies, waits for them, and re-layouts  1.77 us (3%)
    pallas_call x1, Pallas kernels, body(): pl.pallas_call(functools.partial(kernel, length, chunks), out_shape=jax.S...  66.3 us
    unnamed x1, local copies, waits for them, and re-layouts  1.77 us

profile of v1, /device:TPU:0, one launch (start us, length us, event | category | flops | bytes accessed | tf_op | source)
XLA Modules:
  0.0 68.1 jit_solution(5603148356527126529)
XLA Ops:
  0.0 66.3 %shard_map.82 = bf16[1,192,1024]{2,1,0:T(8,128)(2,1)} custom-call(bf16[1,192,1024]{2,1,0:T(8,128)(2,1)} %micro.1, s32[1,192]{1,0:T(1,128)} %ids.1, bf16[1,1024]{1,0:T(2,128)(2,1)} %gain_hbm.1, bf16[192,512]{1,0:T(8,128)(2,1)} %constant.2.clone.table_hbm, bf16[1,1024,2048]{2,1,0:T(8,128)(2,1)} %wq.1, bf16[1,1024,1024]{2,1,0:T(8,128)(2,1)} %wk.1, ...), custom_call_target="tpu_custom_call" | custom-call | tf_op jit(solution)/shard_map/pallas_call | solution.py:221
  66.3 1.8 %copy.10 = bf16[1,192,1024]{2,1,0:T(8,128)(2,1)} copy(bf16[1,192,1024]{2,1,0:T(8,128)(2,1)} %shard_map.82) | data formatting | bytes 786432

commit v2 on v1

--- a/solution.py
+++ b/solution.py
@@ -13,7 +13,7 @@
 KV_HEADS = 8
 HD = 128
 TICKS = 4
-CUT = 96
+PIECES = 4
 BAND = 96
 MESH = pl.DeviceIdType.MESH
 GROUP = 4 * HD
@@ -30,10 +30,9 @@
 
 
 def blocks_of(start, stop):
-    if start == 0:
-        return [(0, stop, 0, stop)]
     rows = 128 - BAND
-    return [(r, r + rows, r - BAND, r + rows) for r in range(start, stop, rows)]
+    later = [(r, r + rows, r - BAND, r + rows) for r in range(128, stop, rows)]
+    return [(0, 128, 0, 128)] + later
 
 
 def kernel(
@@ -80,10 +79,11 @@
     for copy in small:
         copy.wait()
 
-    def rows_copy(t, c):
-        at = pl.ds(chunks[c][0], chunks[c][1] - chunks[c][0])
+    def piece_copy(t, c):
+        width = ybuf.shape[2] // PIECES
+        at = pl.ds(c * width, width)
         return pltpu.make_async_remote_copy(
-            ybuf.at[t, at, :], xbuf.at[t + 1, at, :], send.at[t, c], recv.at[t, c],
+            ybuf.at[t, :, at], xbuf.at[t + 1, :, at], send.at[t, c], recv.at[t, c],
             device_id={"section": right}, device_id_type=MESH,
         )
 
@@ -154,7 +154,8 @@
         for c, (start, stop) in enumerate(chunks):
             rows = pl.ds(start, stop - start)
             if not first:
-                rows_copy(t - 1, c).wait_recv()
+                for piece in range(PIECES):
+                    piece_copy(t - 1, piece).wait_recv()
             x = xbuf[t, rows, :].astype(jnp.float32)
             scale = lax.rsqrt(jnp.mean(x * x, axis=1, keepdims=True) + 1e-05)
             normed[rows, :] = (x * scale * gain[...].astype(jnp.float32)).astype(jnp.bfloat16)
@@ -183,18 +184,19 @@
             attend(KV_HEADS - 1, start, stop)
             if load:
                 out_copy.wait()
-            width = 256
-            for at in range(0, ybuf.shape[2], width):
+            width = ybuf.shape[2] // PIECES
+            for piece in range(PIECES):
+                at = piece * width
                 update = jnp.dot(
                     mixed[rows, :], wout[:, at : at + width], preferred_element_type=jnp.float32
                 )
                 ybuf[t, rows, at : at + width] = (
                     xbuf[t, rows, at : at + width].astype(jnp.float32) + update
                 ).astype(jnp.bfloat16)
-            if first:
-                rows_copy(t, c).start()
-            else:
-                pl.when(t < TICKS - 1)(rows_copy(t, c).start)
+                if first:
+                    piece_copy(t, piece).start()
+                else:
+                    pl.when(t < TICKS - 1)(piece_copy(t, piece).start)
 
     tick(0, True, True)
 
@@ -206,16 +208,15 @@
     out[0] = ybuf[TICKS - 1]
     for t in range(TICKS - 1):
         id_copy(t).wait_send()
-        for c in range(len(chunks)):
-            rows_copy(t, c).wait_send()
+        for piece in range(PIECES):
+            piece_copy(t, piece).wait_send()
 
 
 def body(micro, segment, gain, w_query, w_key, w_value, w_out):
     _, length, width = micro.shape
-    chunks = [(0, CUT), (CUT, length)]
+    chunks = [(0, length)]
     table = jnp.asarray(rope_table(length))
     bf, f32 = jnp.bfloat16, jnp.float32
-    count = len(chunks)
     any_space = pl.BlockSpec(memory_space=pl.ANY)
     vmem = pl.BlockSpec(memory_space=pltpu.VMEM)
     return pl.pallas_call(
@@ -242,8 +243,8 @@
             pltpu.SemaphoreType.DMA((KV_HEADS, 3)),
             pltpu.SemaphoreType.DMA,
             pltpu.SemaphoreType.DMA((4,)),
-            pltpu.SemaphoreType.DMA((TICKS - 1, count)),
-            pltpu.SemaphoreType.DMA((TICKS - 1, count)),
+            pltpu.SemaphoreType.DMA((TICKS - 1, PIECES)),
+            pltpu.SemaphoreType.DMA((TICKS - 1, PIECES)),
             pltpu.SemaphoreType.DMA((TICKS - 1,)),
             pltpu.SemaphoreType.DMA((TICKS - 1,)),
         ],

time: 68.2 us -> 53.6 us (0.79)
  Pallas kernels: 66.3 us -> 51.7 us
    pallas_call x1, Pallas kernels: 66.3 us -> 51.7 us  [body(): pl.pallas_call(functools.partial(kernel, length, chunks), out_shape=jax.S...]
where the time goes in v2:
time: 53.6 us; the launch traced here: 53.4 us
  Pallas kernels  51.7 us (96%)
  local copies, waits for them, and re-layouts  1.77 us (3%)
    pallas_call x1, Pallas kernels, body(): pl.pallas_call(functools.partial(kernel, length, chunks), out_shape=jax.S...  51.7 us
    unnamed x1, local copies, waits for them, and re-layouts  1.77 us

profile of v2, /device:TPU:0, one launch (start us, length us, event | category | flops | bytes accessed | tf_op | source)
XLA Modules:
  0.0 53.4 jit_solution(10210169342743742458)
XLA Ops:
  0.0 51.7 %shard_map.82 = bf16[1,192,1024]{2,1,0:T(8,128)(2,1)} custom-call(bf16[1,192,1024]{2,1,0:T(8,128)(2,1)} %micro.1, s32[1,192]{1,0:T(1,128)} %ids.1, bf16[1,1024]{1,0:T(2,128)(2,1)} %gain_hbm.1, bf16[192,512]{1,0:T(8,128)(2,1)} %constant.2.clone.table_hbm, bf16[1,1024,2048]{2,1,0:T(8,128)(2,1)} %wq.1, bf16[1,1024,1024]{2,1,0:T(8,128)(2,1)} %wk.1, ...), custom_call_target="tpu_custom_call" | custom-call | tf_op jit(solution)/shard_map/pallas_call | solution.py:222
  51.7 1.8 %copy.10 = bf16[1,192,1024]{2,1,0:T(8,128)(2,1)} copy(bf16[1,192,1024]{2,1,0:T(8,128)(2,1)} %shard_map.82) | data formatting | bytes 786432
